TPU v7x, 768 devices: a whole 4x8x12 slice. The times are simulated.
768 devices in a mesh: depth: 8 (over y), row: 2 (over core), col: 48 (over z, x).
Axes of the slice: x: 4, y: 8, z: 12, core: 2. Of those that a mesh axis runs over, the one named last changes fastest.
Arguments:
- density: float32 [128, 256, 6144], P('depth', 'row', 'col'), may hold values from 0.002 to 0.05
- albedo: bfloat16 [3, 128, 256, 6144], P(None, 'depth', 'row', 'col'), may hold values from 0.099609375 to 1
- targets: int32 [2, 8, 2, 48], P(None, None, 'row'), may hold values from -1 to 50, as said below
- offsets: int32 [2, 8, 2, 48], P(None, None, 'row', 'col'), may hold values from 0 to 127
- slab_order: int32 [2, 8], replicated, may hold values from 0 to 7, each once within a row
Outputs:
- frame: float32 [2, 4, 2, 128, 6144], P(None, None, 'row', 'depth', 'col')
Inputs may be any that keep to these rules, and one draw needn't show every extreme that they name: `targets`: within one view and one row and column c of bricks, the 8 values are c + b, c + b, c + b + 1, c + b + 1, ... assigned to the slabs in some order (two bricks for each value, b is -1 or 0; b is -1 in column 0 and 0 in the last column), so one column of bricks sends at most 4 pieces to one screen tile, a number reached in every view, row and column, and only to tiles c - 1 .. c + 4.
All inputs are finite; a program needn't handle non-finite values.
Results may differ from a plain program's by a relative error of at most 0.0015.
Values may be sent and summed in bfloat16 or wider, within the bound.
A program may use at most 32 MiB of HBM per device.

v0:
```python
import math

import jax
import jax.numpy as jnp
from jax import lax
from jax.sharding import PartitionSpec as P

SHEARS = (0.3125, -0.4375)
BRIGHTNESS = 4.0


def sent_to_all(shard, axis):
    copies = jnp.broadcast_to(shard, (lax.axis_size(axis), *shard.shape))
    return lax.all_to_all(copies, axis, split_axis=0, concat_axis=0, tiled=True)


def combined_pairwise(pieces, combine):
    while len(jax.tree.leaves(pieces)[0]) > 1:
        pieces = jax.vmap(combine)(*(pieces[side::2] for side in (0, 1)))
    return pieces[0]


def entering(shard, axis, combine, identity):
    peers, mine = (lax.axis_size(axis), lax.axis_index(axis))
    passed = jnp.arange(peers) < mine

    def kept(part, zero, own):
        part = jnp.where(
            passed.reshape(-1, *(1 for _ in own.shape)), part, jnp.asarray(zero, own.dtype)
        )
        return part

    pieces = sent_to_all(shard, axis)
    return combined_pairwise(kept(pieces, identity, shard), combine)


def shifted(value, axis, steps):
    count = lax.axis_size(axis)
    first, last = (max(0, -steps), min(count, count - steps))
    return lax.ppermute(value, axis, [(source, source + steps) for source in range(first, last)])


def shear_columns(values, shear, plane_index, margin):
    integer_part = math.floor(shear * plane_index)
    fraction = shear * plane_index - integer_part
    col_count = values.shape[-1]
    padding = [(0, 0)] * (values.ndim - 1) + [(margin, margin)]
    padded = jnp.pad(values, padding)
    nearer = padded[..., margin - integer_part : margin - integer_part + col_count]
    farther = padded[..., margin - integer_part - 1 : margin - integer_part - 1 + col_count]
    return (1.0 - fraction) * nearer + fraction * farther


def composite_brick(colour, opacity, shear):
    depth_cells = opacity.shape[0]
    colour_sum = jnp.zeros((3,) + opacity.shape[1:], jnp.float32)
    transmit = jnp.ones(opacity.shape[1:], jnp.float32)
    for plane_index in range(depth_cells):
        moved_colour = shear_columns(colour[:, plane_index], shear, plane_index, depth_cells + 2)
        moved_opacity = shear_columns(opacity[plane_index], shear, plane_index, depth_cells + 2)
        colour_sum = colour_sum + transmit[None] * moved_colour
        transmit = transmit * (1.0 - moved_opacity)
    return jnp.concatenate(
        [colour_sum.astype(jnp.bfloat16), (1.0 - transmit).astype(jnp.bfloat16)[None]], axis=0
    )


def multiply_planes(earlier, later_plane):
    return earlier * later_plane


def route_tables(row_targets, slab_order, slot_count):
    view_count, slabs, columns = row_targets.shape
    window = slabs // 2 + 2
    column_ids = jnp.arange(columns, dtype=jnp.int32)
    relative = row_targets.transpose(0, 2, 1) - column_ids[None, :, None]
    step_ids = jnp.arange(window, dtype=jnp.int32) - 1
    halves = jnp.arange(2, dtype=jnp.int32)
    covers = (
        relative[:, :, None, :, None] + halves[None, None, None, None, :]
        == step_ids[None, None, :, None, None]
    ).astype(jnp.int32)
    covers = covers.reshape(view_count, columns, window, slabs * 2)
    slot_index = jnp.cumsum(covers, axis=-1) - covers
    slot_ids = jnp.arange(slot_count, dtype=jnp.int32)
    selection = covers[:, :, :, None, :] * (
        slot_index[:, :, :, None, :] == slot_ids[None, None, None, :, None]
    ).astype(jnp.int32)
    slab_ids = jnp.arange(slabs, dtype=jnp.int32)
    positions = jnp.sum(
        slab_ids[None, :, None]
        * (slab_order[:, :, None] == slab_ids[None, None, :]).astype(jnp.int32),
        axis=1,
    )
    brick_keys = positions[:, None, :] * columns + column_ids[None, :, None]
    half_keys = (brick_keys[..., None] * jnp.ones((2,), jnp.int32)).reshape(
        view_count, columns, slabs * 2
    )
    source_keys = jnp.sum(selection * half_keys[:, :, None, None, :], axis=-1)
    return (selection.reshape(view_count, columns, window, slot_count, slabs, 2), source_keys)


def placement_table(column_offsets, brick_cols):
    source_cols = jnp.arange(brick_cols, dtype=jnp.int32)
    target_cols = jnp.arange(2 * brick_cols, dtype=jnp.int32).reshape(2, brick_cols)
    landing = source_cols[None, None, :] + column_offsets[:, :, None]
    hits = landing[:, :, :, None, None] == target_cols[None, None, None, :, :]
    return hits.astype(jnp.bfloat16)


def on_device(density, albedo, targets, offsets, slab_order):
    depth_cells, brick_rows, brick_cols = density.shape
    view_count = slab_order.shape[0]
    slabs = lax.axis_size("depth")
    columns = lax.axis_size("col")
    slot_count = min(4, slabs)
    strip_rows = brick_rows // slabs
    window = slabs // 2 + 2
    slab_plane = jnp.exp(-jnp.sum(density, axis=0))
    incoming = entering(slab_plane, "depth", multiply_planes, jnp.ones_like(slab_plane))
    in_front = jnp.cumsum(density, axis=0) - density
    lighting = incoming[None] * jnp.exp(-in_front)
    opacity = 1.0 - jnp.exp(-density)
    colour = BRIGHTNESS * albedo.astype(jnp.float32) * (lighting * opacity)[None]
    brick_images = jnp.stack(
        [composite_brick(colour, opacity, SHEARS[view_index]) for view_index in range(view_count)]
    )
    strips = lax.all_to_all(brick_images[:, None], "depth", split_axis=3, concat_axis=1, tiled=True)
    column_offsets = offsets[:, :, 0, 0]
    placement = placement_table(column_offsets, brick_cols)
    shaped = jnp.einsum(
        "vdkrx,vdxhy->vdkrhy", strips, placement, preferred_element_type=jnp.float32
    ).astype(jnp.bfloat16)
    selection, source_keys = route_tables(targets[:, :, 0, :], slab_order, slot_count)
    my_col = lax.axis_index("col")
    received = []
    key_list = []
    own_table = lax.dynamic_index_in_dim(selection, my_col, axis=1, keepdims=False)
    outgoing = jnp.einsum(
        "vwsdh,vdkrhx->wvskrx",
        own_table.astype(jnp.bfloat16),
        shaped,
        preferred_element_type=jnp.float32,
    ).astype(jnp.bfloat16)
    for step_index in range(window):
        step = step_index - 1
        if step == 0:
            arrived = outgoing[step_index]
        else:
            arrived = shifted(outgoing[step_index], "col", step)
        received.append(arrived)
    for step_index in range(window):
        step = step_index - 1
        source = jnp.clip(my_col - step, 0, columns - 1)
        key_list.append(
            lax.dynamic_index_in_dim(source_keys, source, axis=1, keepdims=False)[:, step_index]
        )
    flat = jnp.stack(received, axis=1).reshape(
        view_count, window * slot_count, 4, strip_rows * brick_cols
    )
    slot_keys = jnp.stack(key_list, axis=1).reshape(view_count, window * slot_count)
    log_transmit = jnp.log1p(-flat[:, :, 3].astype(jnp.float32))
    before = (slot_keys[:, None, :] < slot_keys[:, :, None]).astype(jnp.float32)
    prefix = jnp.einsum("vij,vjx->vix", before, log_transmit, precision=lax.Precision.HIGHEST)
    weight = jnp.exp(prefix)
    colour_sum = jnp.einsum(
        "vikx,vix->vkx", flat[:, :, :3].astype(jnp.float32), weight, precision=lax.Precision.HIGHEST
    )
    frame_opacity = 1.0 - jnp.exp(jnp.sum(log_transmit, axis=1))
    frame = jnp.concatenate([colour_sum, frame_opacity[:, None]], axis=1)
    return frame.reshape(view_count, 4, 1, strip_rows, brick_cols)


def solution(mesh):
    in_specs = (
        P("depth", "row", "col"),
        P(None, "depth", "row", "col"),
        P(None, None, "row", None),
        P(None, None, "row", "col"),
        P(),
    )
    out_specs = P(None, None, "row", "depth", "col")
    return jax.shard_map(
        on_device, mesh=mesh, in_specs=in_specs, out_specs=out_specs, check_vma=False
    )
```

profile of v0, /device:TPU:196, one launch (start us, length us, event | category | flops | bytes accessed | tf_op | source)
XLA Modules:
  0.0 89.3 jit_solution(16150920928950378933)
XLA Ops:
  0.0 1.4 %fusion.350 = (f32[128,128]{1,0:T(8,128)S(1)}, f32[16,128,128]{2,1,0:T(8,128)S(1)}) fusion(f32[16,128,128]{2,1,0:T(8,128)} %param.5), kind=kLoop, calls=%fused_computation.528 | loop fusion | flops 770048 | bytes 2162688 | tf_op jit(solution)/shard_map/reduce_sum | solution.py:119
  1.4 0.8 broadcast_in_dim.21
  2.2 7.1 %all-to-all-start = ((f32[8,128,128]{2,1,0:T(8,128)}), f32[8,128,128]{2,1,0:T(8,128)S(1)}, u32[]{:S(2)}, u32[]{:S(2)}) async-start(f32[8,128,128]{2,1,0:T(8,128)} %broadcast_in_dim.21), calls=%async_computation | async-start | bytes 1048576 | tf_op jit(solution)/shard_map/all_to_all | solution.py:14
  9.4 1.0 %broadcast_multiply_fusion = (f32[128,128]{1,0:T(8,128)}, f32[128,128]{1,0:T(8,128)S(1)}, f32[128,128]{1,0:T(8,128)}, f32[128,128]{1,0:T(8,128)}, f32[128,128]{1...) fusion(f32[128,128]{1,0:T(8,128)S(1)} %get-tuple-element.69, ...), kind=kLoop, calls=%fused_computation.498 | loop fusion | flops 638976 | bytes 1048576 | tf_op jit(solution)/shard_map/mul | solution.py:61
  10.5 1.0 %broadcast_multiply_fusion.1 = (f32[128,128]{1,0:T(8,128)}, f32[128,128]{1,0:T(8,128)S(1)}, f32[128,128]{1,0:T(8,128)}, f32[128,128]{1,0:T(8,128)}, f32[128,128]...) fusion(f32[128,128]{1,0:T(8,128)S(1)} %get-tuple-element.69, ...), kind=kLoop, calls=%fused_computation.499 | loop fusion | flops 638976 | bytes 1048576 | tf_op jit(solution)/shard_map/mul | solution.py:61
  11.5 1.1 %fusion.317 = (bf16[1,128,128]{2,1,0:T(8,128)(2,1)S(1)}, f32[128,128]{1,0:T(8,128)}, f32[128,128]{1,0:T(8,128)}, f32[128,128]{1,0:T(8,128)}, f32[128,128]{1,0:T(...) fusion(f32[128,128]{1,0:T(8,128)S(1)} %get-tuple-element.76, ...), kind=kLoop, calls=%fused_computation.500 | loop fusion | flops 753664 | bytes 1146880 | tf_op jit(solution)/shard_map/broadcast_in_dim | solution.py:64
  12.6 1.1 %fusion.318 = (bf16[1,128,128]{2,1,0:T(8,128)(2,1)S(1)}, f32[128,128]{1,0:T(8,128)}, f32[128,128]{1,0:T(8,128)}, f32[128,128]{1,0:T(8,128)}, f32[128,128]{1,0:T(...) fusion(f32[128,128]{1,0:T(8,128)S(1)} %get-tuple-element.76, ...), kind=kLoop, calls=%fused_computation.501 | loop fusion | flops 753664 | bytes 1146880 | tf_op jit(solution)/shard_map/broadcast_in_dim | solution.py:64
  14.1 2.2 %reduce_window_sum.26 = s32[2,48,6,1,16]{4,1,2,3,0:T(8,128)S(1)} reduce-window(s32[2,48,6,1,16]{4,1,2,3,0:T(8,128)S(1)} %compare_convert_fusion, s32[]{:T(128)} %constant.36.clone.1), window={size=1x1x1x1x16 pad=0_0x0_0x0_0x0_0x15_0}, to_apply=%region_0.0 | reduce-window | flops 138240 | bytes 73732 | tf_op jit(solution)/shard_map/jit(cumsum)/reduce_window_sum | solution.py:84
  17.1 0.7 copy.257
  17.8 0.7 copy.265
  18.5 0.7 copy.266
  19.2 0.8 select_reduce_fusion
  20.0 1.3 %iota_add_fusion.1 = s32[2,8,128]{2,1,0:T(8,128)} fusion(s32[2,8]{1,0:T(2,128)} %bitcast.207), kind=kLoop, calls=%fused_computation.508 | loop fusion | flops 2048 | bytes 8256 | tf_op jit(solution)/shard_map/add | solution.py:106
  21.4 0.7 iota_add_fusion.2
  22.0 4.8 %all-to-all-done = f32[8,128,128]{2,1,0:T(8,128)S(1)} async-done(((f32[8,128,128]{2,1,0:T(8,128)}), f32[8,128,128]{2,1,0:T(8,128)S(1)}, u32[]{:S(2)}, u32[]{:S(2)}) %all-to-all-start) | async-done | bytes 524320 | tf_op jit(solution)/shard_map/all_to_all | solution.py:14
  26.8 0.7 broadcast_select_fusion
  28.0 1.0 %copy-done.1 = bf16[3,16,128,128]{3,2,1,0:T(8,128)(2,1)S(1)} copy-done((bf16[3,16,128,128]{3,2,1,0:T(8,128)(2,1)S(1)}, bf16[3,16,128,128]{3,2,1,0:T(8,128)(2,1)}, u32[]{:S(2)}) %copy-start.1) | copy-done | bytes 1572888
  28.9 1.8 %convert_multiply_fusion = f32[3,16,128,128]{3,0,2,1:T(4,128)S(1)} fusion(bf16[3,16,128,128]{3,2,1,0:T(8,128)(2,1)S(1)} %copy-done.1, f32[16,128,128]{2,1,0:T(8,128)S(1)} %multiply_multiply_fusion), kind=kLoop, calls=%fused_computation | loop fusion | flops 1572864 | bytes 5767168 | tf_op jit(solution)/shard_map/mul | solution.py:124
  30.9 1.2 %slice_bitcast_fusion.16 = (f32[3,128,128]{2,0,1:T(4,128)S(1)}, f32[3,128,128]{2,0,1:T(4,128)S(1)}, f32[3,128,128]{2,0,1:T(4,128)S(1)}, f32[3,128,128]{2,0,1:T(4...) fusion(f32[3,16,128,128]{3,0,2,1:T(4,128)S(1)} %convert_multipl, ...), kind=kLoop, calls=%fused_computation.239 | loop fusion | bytes 6291456 | tf_op jit(solution)/shard_map/squeeze | solution.py:59
  32.4 4.3 %fusion.162 = bf16[3,128,128]{2,0,1:T(4,128)(2,1)S(1)} fusion(f32[3,128,128]{2,0,1:T(4,128)S(1)} %get-tuple-element.38, f32[3,128,128]{2,0,1:T(4,128)S(1)} %get-tuple-element.39, f32[3,128,128]{2,0,1:T(4,128)S(1)} %get-tuple-element.40, f32[3,128,128]{2,0,1:T(4,128)S(1)} %get-tuple-element.41, f32[3,128,128]{2,0,1:T(4,128)S(1)} %get-tuple-element.42, ...), kind=kLoop, calls=%fused_computation.245 | loop fusion | flops 3735552 | bytes 4227072 | tf_op jit(solution)/shard_map/convert_element_type | solution.py:64
  36.8 4.2 %fusion.163 = bf16[3,128,128]{2,0,1:T(4,128)(2,1)S(1)} fusion(f32[3,128,128]{2,0,1:T(4,128)S(1)} %get-tuple-element.38, f32[3,128,128]{2,0,1:T(4,128)S(1)} %get-tuple-element.39, f32[3,128,128]{2,0,1:T(4,128)S(1)} %get-tuple-element.40, f32[3,128,128]{2,0,1:T(4,128)S(1)} %get-tuple-element.41, f32[3,128,128]{2,0,1:T(4,128)S(1)} %get-tuple-element.42, ...), kind=kLoop, calls=%fused_computation.246 | loop fusion | flops 3735552 | bytes 4227072 | tf_op jit(solution)/shard_map/convert_element_type | solution.py:64
  41.3 0.9 maximum_bitcast_fusion
  42.2 3.4 %all-to-all-start.1 = ((bf16[2,1,4,128,128]{4,2,0,1,3:T(4,128)(2,1)}), bf16[2,1,4,128,128]{4,2,0,1,3:T(4,128)(2,1)S(1)}, u32[]{:S(2)}, u32[]{:S(2)}) async-start(bf16[2,1,4,128,128]{4,2,0,1,3:T(4,128)(2,1)} %maximum_bitcast_fusion), calls=%async_computation.1 | async-start | bytes 524288 | tf_op jit(solution)/shard_map/all_to_all | solution.py:128
  45.8 12.1 %all-to-all-done.1 = bf16[2,1,4,128,128]{4,2,0,1,3:T(4,128)(2,1)S(1)} async-done(((bf16[2,1,4,128,128]{4,2,0,1,3:T(4,128)(2,1)}), bf16[2,1,4,128,128]{4,2,0,1,3:T(4,128)(2,1)S(1)}, u32[]{:S(2)}, u32[]{:S(2)}) %all-to-all-start.1) | async-done | bytes 262176 | tf_op jit(solution)/shard_map/all_to_all | solution.py:128
  59.0 1.6 %fusion.349 = (bf16[1,2,4,4,16,128]{5,0,2,4,3,1:T(2,128)(2,1)S(1)}, bf16[1,2,4,4,16,128]{5,0,2,4,3,1:T(2,128)(2,1)S(1)}, bf16[1,2,4,4,16,128]{5,0,2,4,3,1:T(2,12...) fusion(bf16[6,2,4,4,16,128]{5,0,2,4,3,1:T(8,128)(2,1)S(1)} %fus, ...), kind=kLoop, calls=%fused_computation.527 | loop fusion | bytes 1572864 | tf_op jit(solution)/shard_map/slice | solution.py:150
  60.6 2.6 %collective-permute-start = (bf16[2,4,4,16,128]{4,3,2,1,0:T(8,128)(2,1)S(1)}, bf16[2,4,4,16,128]{4,3,2,1,0:T(8,128)(2,1)S(1)}, u32[]{:S(2)}, u32[]{:S(2)}) collective-permute-start(bf16[2,4,4,16,128]{4,3,2,1,0:T(8,128)(2,1)S(1)} %bitcast.192), channel_id=1, source_target_pairs={{1,0},{2,1},{3,2},{4,3},{5,4},{6,5},{7,6},{8,7},{9,8},{10,9},{11,1... | collective-permute-start | bytes 393224 | tf_op jit(solution)/shard_map/ppermute | solution.py:40
  65.1 3.4 %collective-permute-start.1 = (bf16[2,4,4,16,128]{4,3,2,1,0:T(8,128)(2,1)S(1)}, bf16[2,4,4,16,128]{4,3,2,1,0:T(8,128)(2,1)S(1)}, u32[]{:S(2)}, u32[]{:S(2)}) collective-permute-start(bf16[2,4,4,16,128]{4,3,2,1,0:T(8,128)(2,1)S(1)} %bitcast.196), channel_id=1, source_target_pairs={{0,1},{1,2},{2,3},{3,4},{4,5},{5,6},{6,7},{7,8},{8,9},{9,10},{10,1... | collective-permute-start | bytes 393224 | tf_op jit(solution)/shard_map/ppermute | solution.py:40
  68.5 5.4 %collective-permute-start.2 = (bf16[2,4,4,16,128]{4,3,2,1,0:T(8,128)(2,1)S(1)}, bf16[2,4,4,16,128]{4,3,2,1,0:T(8,128)(2,1)S(1)}, u32[]{:S(2)}, u32[]{:S(2)}) collective-permute-start(bf16[2,4,4,16,128]{4,3,2,1,0:T(8,128)(2,1)S(1)} %bitcast.195), channel_id=1, source_target_pairs={{0,2},{1,3},{2,4},{3,5},{4,6},{5,7},{6,8},{7,9},{8,10},{9,11},{10,... | collective-permute-start | bytes 393224 | tf_op jit(solution)/shard_map/ppermute | solution.py:40
  74.0 6.2 %collective-permute-start.3 = (bf16[2,4,4,16,128]{4,3,2,1,0:T(8,128)(2,1)S(1)}, bf16[2,4,4,16,128]{4,3,2,1,0:T(8,128)(2,1)S(1)}, u32[]{:S(2)}, u32[]{:S(2)}) collective-permute-start(bf16[2,4,4,16,128]{4,3,2,1,0:T(8,128)(2,1)S(1)} %bitcast.194), channel_id=1, source_target_pairs={{0,3},{1,4},{2,5},{3,6},{4,7},{5,8},{6,9},{7,10},{8,11},{9,12},{10... | collective-permute-start | bytes 393224 | tf_op jit(solution)/shard_map/ppermute | solution.py:40
  80.2 4.3 %collective-permute-start.4 = (bf16[2,4,4,16,128]{4,3,2,1,0:T(8,128)(2,1)S(1)}, bf16[2,4,4,16,128]{4,3,2,1,0:T(8,128)(2,1)S(1)}, u32[]{:S(2)}, u32[]{:S(2)}) collective-permute-start(bf16[2,4,4,16,128]{4,3,2,1,0:T(8,128)(2,1)S(1)} %bitcast.193), channel_id=1, source_target_pairs={{0,4},{1,5},{2,6},{3,7},{4,8},{5,9},{6,10},{7,11},{8,12},{9,13},{1... | collective-permute-start | bytes 393224 | tf_op jit(solution)/shard_map/ppermute | solution.py:40
  84.7 2.4 %collective-permute-done.4 = bf16[2,4,4,16,128]{4,3,2,1,0:T(8,128)(2,1)S(1)} collective-permute-done((bf16[2,4,4,16,128]{4,3,2,1,0:T(8,128)(2,1)S(1)}, bf16[2,4,4,16,128]{4,3,2,1,0:T(8,128)(2,1)S(1)}, u32[]{:S(2)}, u32[]{:S(2)}) %collective-permute-start.4) | collective-permute-done | bytes 131104 | tf_op jit(solution)/shard_map/ppermute | solution.py:40
  88.7 0.6 copy.276
  (142 shorter events, 7.0 us)
Async XLA Ops:
  2.2 24.6 %all-to-all-start = ((f32[8,128,128]{2,1,0:T(8,128)}), f32[8,128,128]{2,1,0:T(8,128)S(1)}, u32[]{:S(2)}, u32[]{:S(2)}) async-start(f32[8,128,128]{2,1,0:T(8,128)} %broadcast_in_dim.21), calls=%async_computation | async-start | bytes 1048576 | tf_op jit(solution)/shard_map/all_to_all | solution.py:14
  9.4 4.3 %copy-start.35 = (s32[2,8,1,48]{3,2,1,0:T(1,128)S(1)}, s32[2,8,1,48]{3,2,1,0:T(1,128)}, u32[]{:S(2)}) copy-start(s32[2,8,1,48]{3,2,1,0:T(1,128)} %param.7) | copy-start | bytes 9220
  11.5 5.6 %copy-start.32 = (s32[6]{0:T(128)}, s32[6]{0:T(128)S(1)}, u32[]{:S(2)}) copy-start(s32[6]{0:T(128)S(1)} %iota_add_fusion.3) | copy-start | bytes 76
  17.8 9.8 %copy-start = (f32[16,128,128]{2,1,0:T(8,128)S(1)}, f32[16,128,128]{2,1,0:T(8,128)}, u32[]{:S(2)}) copy-start(f32[16,128,128]{2,1,0:T(8,128)} %param.5) | copy-start | bytes 3145732
  27.5 1.4 %copy-start.1 = (bf16[3,16,128,128]{3,2,1,0:T(8,128)(2,1)S(1)}, bf16[3,16,128,128]{3,2,1,0:T(8,128)(2,1)}, u32[]{:S(2)}) copy-start(bf16[3,16,128,128]{3,2,1,0:T(8,128)(2,1)} %param.6) | copy-start | bytes 4718596
  30.8 1.3 %copy-start.10 = (f32[128,128]{1,0:T(8,128)S(1)}, f32[128,128]{1,0:T(8,128)}, u32[]{:S(2)}) copy-start(f32[128,128]{1,0:T(8,128)} %get-tuple-element.21) | copy-start | bytes 196612
  30.8 1.3 %copy-start.11 = (f32[128,128]{1,0:T(8,128)S(1)}, f32[128,128]{1,0:T(8,128)}, u32[]{:S(2)}) copy-start(f32[128,128]{1,0:T(8,128)} %get-tuple-element.23) | copy-start | bytes 196612
  30.8 1.3 %copy-start.12 = (f32[128,128]{1,0:T(8,128)S(1)}, f32[128,128]{1,0:T(8,128)}, u32[]{:S(2)}) copy-start(f32[128,128]{1,0:T(8,128)} %get-tuple-element.24) | copy-start | bytes 196612
  32.2 4.5 %copy-start.3 = (f32[128,128]{1,0:T(8,128)S(1)}, f32[128,128]{1,0:T(8,128)}, u32[]{:S(2)}) copy-start(f32[128,128]{1,0:T(8,128)} %get-tuple-element.5) | copy-start | bytes 196612
  32.2 4.5 %copy-start.4 = (f32[128,128]{1,0:T(8,128)S(1)}, f32[128,128]{1,0:T(8,128)}, u32[]{:S(2)}) copy-start(f32[128,128]{1,0:T(8,128)} %get-tuple-element.7) | copy-start | bytes 196612
  32.2 4.5 %copy-start.5 = (f32[128,128]{1,0:T(8,128)S(1)}, f32[128,128]{1,0:T(8,128)}, u32[]{:S(2)}) copy-start(f32[128,128]{1,0:T(8,128)} %get-tuple-element.8) | copy-start | bytes 196612
  32.3 4.5 %copy-start.6 = (f32[128,128]{1,0:T(8,128)S(1)}, f32[128,128]{1,0:T(8,128)}, u32[]{:S(2)}) copy-start(f32[128,128]{1,0:T(8,128)} %get-tuple-element.9) | copy-start | bytes 196612
  32.3 4.5 %copy-start.7 = (f32[128,128]{1,0:T(8,128)S(1)}, f32[128,128]{1,0:T(8,128)}, u32[]{:S(2)}) copy-start(f32[128,128]{1,0:T(8,128)} %get-tuple-element.10) | copy-start | bytes 196612
  32.3 4.5 %copy-start.8 = (f32[128,128]{1,0:T(8,128)S(1)}, f32[128,128]{1,0:T(8,128)}, u32[]{:S(2)}) copy-start(f32[128,128]{1,0:T(8,128)} %get-tuple-element.11) | copy-start | bytes 196612
  32.3 4.5 %copy-start.9 = (f32[128,128]{1,0:T(8,128)S(1)}, f32[128,128]{1,0:T(8,128)}, u32[]{:S(2)}) copy-start(f32[128,128]{1,0:T(8,128)} %get-tuple-element.12) | copy-start | bytes 196612
  32.3 4.5 %copy-start.17 = (f32[128,128]{1,0:T(8,128)S(1)}, f32[128,128]{1,0:T(8,128)}, u32[]{:S(2)}) copy-start(f32[128,128]{1,0:T(8,128)} %get-tuple-element.14) | copy-start | bytes 196612
  32.3 4.5 %copy-start.18 = (f32[128,128]{1,0:T(8,128)S(1)}, f32[128,128]{1,0:T(8,128)}, u32[]{:S(2)}) copy-start(f32[128,128]{1,0:T(8,128)} %get-tuple-element.15) | copy-start | bytes 196612
  32.3 4.5 %copy-start.19 = (f32[128,128]{1,0:T(8,128)S(1)}, f32[128,128]{1,0:T(8,128)}, u32[]{:S(2)}) copy-start(f32[128,128]{1,0:T(8,128)} %get-tuple-element.16) | copy-start | bytes 196612
  32.3 4.5 %copy-start.20 = (f32[128,128]{1,0:T(8,128)S(1)}, f32[128,128]{1,0:T(8,128)}, u32[]{:S(2)}) copy-start(f32[128,128]{1,0:T(8,128)} %get-tuple-element.17) | copy-start | bytes 196612
  32.3 4.5 %copy-start.21 = (f32[128,128]{1,0:T(8,128)S(1)}, f32[128,128]{1,0:T(8,128)}, u32[]{:S(2)}) copy-start(f32[128,128]{1,0:T(8,128)} %get-tuple-element.18) | copy-start | bytes 196612
  32.3 4.5 %copy-start.22 = (f32[128,128]{1,0:T(8,128)S(1)}, f32[128,128]{1,0:T(8,128)}, u32[]{:S(2)}) copy-start(f32[128,128]{1,0:T(8,128)} %get-tuple-element.19) | copy-start | bytes 196612
  32.4 4.5 %copy-start.23 = (f32[128,128]{1,0:T(8,128)S(1)}, f32[128,128]{1,0:T(8,128)}, u32[]{:S(2)}) copy-start(f32[128,128]{1,0:T(8,128)} %get-tuple-element.20) | copy-start | bytes 196612
  36.8 4.2 %copy-start.2 = (bf16[1,128,128]{2,0,1:T(2,128)(2,1)S(1)}, bf16[1,128,128]{2,0,1:T(2,128)(2,1)}, u32[]{:S(2)}) copy-start(bf16[1,128,128]{2,0,1:T(2,128)(2,1)} %copy.257) | copy-start | bytes 98308
  36.8 8.8 %copy-start.33 = (s32[6]{0:T(128)S(1)}, s32[6]{0:T(128)}, u32[]{:S(2)}) copy-start(s32[6]{0:T(128)} %copy-done.32) | copy-start | bytes 76
  36.8 21.0 %copy-start.34 = (s32[2,8,128]{2,1,0:T(8,128)S(1)}, s32[2,8,128]{2,1,0:T(8,128)}, u32[]{:S(2)}) copy-start(s32[2,8,128]{2,1,0:T(8,128)} %iota_add_fusion.1) | copy-start | bytes 24580
  42.2 15.7 %all-to-all-start.1 = ((bf16[2,1,4,128,128]{4,2,0,1,3:T(4,128)(2,1)}), bf16[2,1,4,128,128]{4,2,0,1,3:T(4,128)(2,1)S(1)}, u32[]{:S(2)}, u32[]{:S(2)}) async-start(bf16[2,1,4,128,128]{4,2,0,1,3:T(4,128)(2,1)} %maximum_bitcast_fusion), calls=%async_computation.1 | async-start | bytes 524288 | tf_op jit(solution)/shard_map/all_to_all | solution.py:128
  59.0 4.2 %copy-start.31 = (s32[2,48,8]{1,2,0:T(8,128)S(1)}, s32[2,48,8]{1,2,0:T(8,128)}, u32[]{:S(2)}) copy-start(s32[2,48,8]{1,2,0:T(8,128)} %iota_add_fusion.2) | copy-start | bytes 9220
  60.6 23.9 %collective-permute-start = (bf16[2,4,4,16,128]{4,3,2,1,0:T(8,128)(2,1)S(1)}, bf16[2,4,4,16,128]{4,3,2,1,0:T(8,128)(2,1)S(1)}, u32[]{:S(2)}, u32[]{:S(2)}) collective-permute-start(bf16[2,4,4,16,128]{4,3,2,1,0:T(8,128)(2,1)S(1)} %bitcast.192), channel_id=1, source_target_pairs={{1,0},{2,1},{3,2},{4,3},{5,4},{6,5},{7,6},{8,7},{9,8},{10,9},{11,1... | collective-permute-start | bytes 393224 | tf_op jit(solution)/shard_map/ppermute | solution.py:40
  65.1 19.5 %collective-permute-start.1 = (bf16[2,4,4,16,128]{4,3,2,1,0:T(8,128)(2,1)S(1)}, bf16[2,4,4,16,128]{4,3,2,1,0:T(8,128)(2,1)S(1)}, u32[]{:S(2)}, u32[]{:S(2)}) collective-permute-start(bf16[2,4,4,16,128]{4,3,2,1,0:T(8,128)(2,1)S(1)} %bitcast.196), channel_id=1, source_target_pairs={{0,1},{1,2},{2,3},{3,4},{4,5},{5,6},{6,7},{7,8},{8,9},{9,10},{10,1... | collective-permute-start | bytes 393224 | tf_op jit(solution)/shard_map/ppermute | solution.py:40
  68.5 16.1 %collective-permute-start.2 = (bf16[2,4,4,16,128]{4,3,2,1,0:T(8,128)(2,1)S(1)}, bf16[2,4,4,16,128]{4,3,2,1,0:T(8,128)(2,1)S(1)}, u32[]{:S(2)}, u32[]{:S(2)}) collective-permute-start(bf16[2,4,4,16,128]{4,3,2,1,0:T(8,128)(2,1)S(1)} %bitcast.195), channel_id=1, source_target_pairs={{0,2},{1,3},{2,4},{3,5},{4,6},{5,7},{6,8},{7,9},{8,10},{9,11},{10,... | collective-permute-start | bytes 393224 | tf_op jit(solution)/shard_map/ppermute | solution.py:40
  74.0 10.6 %collective-permute-start.3 = (bf16[2,4,4,16,128]{4,3,2,1,0:T(8,128)(2,1)S(1)}, bf16[2,4,4,16,128]{4,3,2,1,0:T(8,128)(2,1)S(1)}, u32[]{:S(2)}, u32[]{:S(2)}) collective-permute-start(bf16[2,4,4,16,128]{4,3,2,1,0:T(8,128)(2,1)S(1)} %bitcast.194), channel_id=1, source_target_pairs={{0,3},{1,4},{2,5},{3,6},{4,7},{5,8},{6,9},{7,10},{8,11},{9,12},{10... | collective-permute-start | bytes 393224 | tf_op jit(solution)/shard_map/ppermute | solution.py:40
  80.2 6.9 %collective-permute-start.4 = (bf16[2,4,4,16,128]{4,3,2,1,0:T(8,128)(2,1)S(1)}, bf16[2,4,4,16,128]{4,3,2,1,0:T(8,128)(2,1)S(1)}, u32[]{:S(2)}, u32[]{:S(2)}) collective-permute-start(bf16[2,4,4,16,128]{4,3,2,1,0:T(8,128)(2,1)S(1)} %bitcast.193), channel_id=1, source_target_pairs={{0,4},{1,5},{2,6},{3,7},{4,8},{5,9},{6,10},{7,11},{8,12},{9,13},{1... | collective-permute-start | bytes 393224 | tf_op jit(solution)/shard_map/ppermute | solution.py:40
  (11 other events, 14.6 us)
where the time goes:
time: 89.8 us; the launch traced here: 89.3 us
  starting transfers between devices  32.4 us (36%)
  other arithmetic  24.7 us (28%)
  waiting for transfers between devices  19.3 us (21%)
  local copies, waits for them, and re-layouts  10.3 us (11%)
  matrix products  1.59 us (2%)
  between operations  1 us (1%)
    ppermute x5, starting transfers between devices, shifted(): lax.ppermute(value, axis, [(source, source + steps) for source in range(f...  21.9 us
    all_to_all x1, waiting for transfers between devices, on_device(): lax.all_to_all(brick_images[:, None], 'depth', split_axis=3, concat_axis=...  12.1 us
    convert_element_type x2, other arithmetic, composite_brick(): colour_sum.astype(jnp.bfloat16)  8.46 us
    all_to_all x1, starting transfers between devices, sent_to_all(): return lax.all_to_all(copies, axis, split_axis=0, concat_axis=0, tiled=True)  7.1 us
    all_to_all x1, waiting for transfers between devices, sent_to_all(): return lax.all_to_all(copies, axis, split_axis=0, concat_axis=0, tiled=True)  4.81 us
    all_to_all x1, starting transfers between devices, on_device(): lax.all_to_all(brick_images[:, None], 'depth', split_axis=3, concat_axis=...  3.41 us
    ppermute x5, waiting for transfers between devices, shifted(): lax.ppermute(value, axis, [(source, source + steps) for source in range(f...  2.4 us
    broadcast_in_dim x2, other arithmetic, composite_brick(): (1.0 - transmit).astype(jnp.bfloat16)[None]  2.23 us
  transfers between devices with their start and end apart: 7, of which 3 were waited for; matrix products, arithmetic and copies ran while one was open for 16% of the time, Pallas kernels for 0%

commit v1 on v0

v1 whole, which is shorter than its diff:
```python
import functools
import math

import jax
import jax.numpy as jnp
from jax import lax
from jax.experimental import pallas as pl
from jax.experimental.pallas import tpu as pltpu
from jax.sharding import PartitionSpec as P

SHEARS = (0.3125, -0.4375)
BRIGHTNESS = 4.0
MESH = pl.DeviceIdType.MESH

STEPS = (-1, 0, 1, 2, 3, 4)
SLOT_COUNT = {-1: 2, 0: 4, 1: 4, 2: 4, 3: 4, 4: 2}
SLOT_BASE = {-1: 0, 0: 2, 1: 6, 2: 10, 3: 14, 4: 18}
SLOTS = 20
EMPTY = 20


def shear_plan(shear, depth_cells):
    plan = []
    for z in range(depth_cells):
        whole = math.floor(shear * z)
        plan.append((whole, shear * z - whole))
    terms = sorted({k + e for k, f in plan for e in (0, 1) if e == 0 or f > 0})
    return plan, terms


def kernel(
    sizes,
    density_hbm,
    albedo_hbm,
    targets,
    offsets,
    slab_order,
    out_ref,
    dens,
    alb,
    depth_strips,
    depth_seen,
    light_strips,
    light,
    partial,
    images,
    strips_a,
    strips_b,
    outgoing,
    landed_a,
    landed_b,
    table,
    load_sems,
    a_send,
    a_recv,
    b_send,
    b_recv,
    y_send,
    y_recv,
    c_send,
    c_recv,
):
    slabs, columns, depth_cells, rows, lanes = sizes
    views = len(SHEARS)
    strips, landed = (strips_a, strips_b), (landed_a, landed_b)
    strip = rows // slabs
    plans = [shear_plan(shear, depth_cells) for shear in SHEARS]
    firsts = [0, len(plans[0][1])]
    me = lax.axis_index("depth")
    col = lax.axis_index("col")

    load_density = pltpu.make_async_copy(density_hbm, dens, load_sems.at[0])
    load_albedo = pltpu.make_async_copy(albedo_hbm, alb, load_sems.at[1])
    load_density.start()
    load_albedo.start()

    barrier = pltpu.get_barrier_semaphore()
    for hop in range(1, slabs):
        pl.semaphore_signal(
            barrier, inc=1, device_id={"depth": lax.rem(me + hop, slabs)}, device_id_type=MESH
        )
    for hop in (-4, -3, -2, -1, 1, 2, 3, 4):

        @pl.when((col + hop >= 0) & (col + hop < columns))
        def _(hop=hop):
            pl.semaphore_signal(
                barrier, inc=1, device_id={"col": col + hop}, device_id_type=MESH
            )

    lane = lax.broadcasted_iota(jnp.int32, (strip, lanes), 1)

    def strip_rows(p):
        return pl.ds(pl.multiple_of(p * strip, strip), strip)

    load_density.wait()

    @pl.loop(0, slabs)
    def _(p):
        depth_strips[p] = jnp.sum(dens[:, strip_rows(p), :], axis=0)

    neighbours = jnp.minimum(col, 4) + jnp.minimum(columns - 1 - col, 4)
    pl.semaphore_wait(barrier, slabs - 1 + neighbours)

    def peer_at(i):
        half, sign = (i + 1) // 2, 1 - 2 * (i % 2)
        return lax.rem(me + slabs // 2 + sign * half, slabs)

    def depth_copy(src, dst, send, recv, slot_send, slot_recv, peer):
        return pltpu.make_async_remote_copy(
            src_ref=src,
            dst_ref=dst,
            send_sem=send.at[slot_send],
            recv_sem=recv.at[slot_recv],
            device_id={"depth": peer},
            device_id_type=MESH,
        )

    def a_copy(peer, source):
        return depth_copy(
            depth_strips.at[peer], depth_seen.at[source], a_send, a_recv, peer, source, peer
        )

    def b_copy(peer, source):
        return depth_copy(
            light_strips.at[peer], light.at[source], b_send, b_recv, peer, source, peer
        )

    @pl.loop(0, slabs - 1)
    def _(i):
        a_copy(peer_at(i), me).start()

    depth_seen[me] = depth_strips[me]
    load_albedo.wait()

    def lane_mask(shift, weight):
        inside = (lane >= shift) if shift >= 0 else (lane < lanes + shift)
        return jnp.where(inside, jnp.float32(weight), jnp.float32(0.0))

    def rolled(value, shift):
        return value if shift % lanes == 0 else pltpu.roll(value, shift % lanes, 1)

    def composite(p):
        at = strip_rows(p)
        inside = jnp.ones((strip, lanes), jnp.float32)
        transmit = [jnp.ones((strip, lanes), jnp.float32) for _ in range(views)]
        sums = [{} for _ in range(views)]
        for z in range(depth_cells):
            through = jnp.exp(-dens[z, at, :])
            opacity = 1.0 - through
            lit = (BRIGHTNESS * inside) * opacity
            inside = inside * through
            colour = [alb[c, z, at, :].astype(jnp.float32) * lit for c in range(3)]
            for v in range(views):
                whole, fraction = plans[v][0][z]
                moved = None
                for k, weight in ((whole, 1.0 - fraction), (whole + 1, fraction)):
                    if weight == 0.0:
                        continue
                    part = lane_mask(k, weight) * rolled(opacity, k)
                    moved = part if moved is None else moved + part
                    seen = transmit[v] if z else None
                    seen = lane_mask(-k, weight) * (
                        rolled(seen, -k) if z else jnp.ones((strip, lanes), jnp.float32)
                    )
                    terms = [seen * colour[c] for c in range(3)]
                    if k in sums[v]:
                        terms = [old + new for old, new in zip(sums[v][k], terms)]
                    sums[v][k] = terms
                transmit[v] = transmit[v] * (1.0 - moved)
                later = {
                    k for w, f in plans[v][0][z + 1 :] for k in ((w, w + 1) if f else (w,))
                }
                for k in [k for k in sums[v] if k not in later]:
                    for c in range(3):
                        partial[firsts[v] + plans[v][1].index(k), c, at, :] = sums[v][k][c]
                    del sums[v][k]
        for v in range(views):
            image = pltpu.roll(1.0 - transmit[v], offsets[v, 0, 0, me], 1)
            images[v, p, 3] = image.astype(jnp.bfloat16)

    early = slabs // 2
    pl.loop(0, early)(composite)

    @pl.loop(0, slabs - 1)
    def _(i):
        a_copy(me, peer_at(i)).wait_recv()

    front = jnp.zeros((strip, lanes), jnp.float32)
    for d in range(slabs):
        light_strips[d] = jnp.exp(-front)
        front = front + depth_seen[d]

    @pl.loop(0, slabs - 1)
    def _(i):
        b_copy(peer_at(i), me).start()

    light[me] = light_strips[me]

    pl.loop(early, slabs)(composite)

    for v in range(views):
        for n, step in enumerate(STEPS):
            source = col - step
            present = (source >= 0) & (source < columns)
            source = jnp.clip(source, 0, columns - 1)
            rel = [targets[v, d, 0, source] - source for d in range(slabs)]
            for d in range(slabs):
                second = functools.reduce(
                    jnp.logical_or, [rel[e] == rel[d] for e in range(d)], False
                )
                member = jnp.where(second, 1, 0)
                slot = jnp.int32(EMPTY)
                if step < 4:
                    slot = jnp.where(rel[d] == step, SLOT_BASE[step] + member, slot)
                if step > -1:
                    after = SLOT_BASE[step] + (2 if step < 4 else 0)
                    slot = jnp.where(rel[d] == step - 1, after + member, slot)
                table[v, n, d] = jnp.where(present, slot, EMPTY)

    @pl.loop(0, slabs - 1)
    def _(i):
        b_copy(me, peer_at(i)).wait_recv()

    def y_copy(v, peer, source):
        return depth_copy(
            images.at[v, peer],
            strips[v].at[source],
            y_send.at[v],
            y_recv.at[v],
            peer,
            source,
            peer,
        )

    for v in range(views):

        @pl.loop(0, slabs)
        def _(i, v=v):
            p = peer_at(i)
            at = strip_rows(p)
            front_light = light[p]
            for c in range(3):
                total = None
                for n, k in enumerate(plans[v][1]):
                    part = rolled(front_light * partial[firsts[v] + n, c, at, :], k)
                    total = part if total is None else total + part
                total = pltpu.roll(total, offsets[v, 0, 0, me], 1)
                images[v, p, c] = total.astype(jnp.bfloat16)

            @pl.when(i < slabs - 1)
            def _():
                y_copy(v, p, me).start()

        strips[v][me] = images[v, me]

    def c_copy(v, step):
        base, count = SLOT_BASE[step], SLOT_COUNT[step]
        n = STEPS.index(step)
        return pltpu.make_async_remote_copy(
            src_ref=outgoing.at[v, pl.ds(base, count)],
            dst_ref=landed[v].at[pl.ds(base, count)],
            send_sem=c_send.at[v, n],
            recv_sem=c_recv.at[v, n],
            device_id={"col": col + step},
            device_id_type=MESH,
        )

    for v in range(views):
        landed[v][EMPTY] = jnp.zeros(landed[v].shape[1:], jnp.bfloat16)

        @pl.loop(0, slabs - 1)
        def _(i, v=v):
            y_copy(v, me, peer_at(i)).wait_recv()

        rel = [targets[v, d, 0, col] - col for d in range(slabs)]
        for step in (3, 2, 1, 0, -1):
            match = [r == step for r in rel]
            first = jnp.int32(slabs)
            second = jnp.int32(-1)
            for d in range(slabs):
                first = jnp.where(match[d], jnp.minimum(first, d), first)
                second = jnp.where(match[d], d, second)
            valid = second >= 0
            for member, slab in ((0, first), (1, second)):
                slab = jnp.where(valid, slab, 0)
                start = offsets[v, 0, 0, slab]
                piece = strips[v][slab]
                left_from = jnp.where(valid, start, lanes)
                right_to = jnp.where(valid, start, 0)
                left = jnp.where(lane >= left_from, 1.0, 0.0).astype(jnp.bfloat16)
                right = jnp.where(lane < right_to, 1.0, 0.0).astype(jnp.bfloat16)
                after = step + 1
                slots_of = [landed[v] if s == 0 else outgoing.at[v] for s in (step, after)]
                slots_of[0][SLOT_BASE[step] + member] = piece * left
                slots_of[1][SLOT_BASE[after] + (2 if after < 4 else 0) + member] = piece * right
            for ready in ((4,) if step == 3 else (step + 1,)) + ((-1,) if step == -1 else ()):
                if ready == 0:
                    continue

                @pl.when((col + ready >= 0) & (col + ready < columns))
                def _(v=v, ready=ready):
                    c_copy(v, ready).start()

    for v in range(views):
        for step in STEPS:
            if step == 0:
                continue

            @pl.when((col - step >= 0) & (col - step < columns))
            def _(v=v, step=step):
                c_copy(v, step).wait_recv()

        def at_position(position, state, v=v):
            slab = slab_order[v, position]
            red, green, blue, transmit = state
            for n in reversed(range(len(STEPS))):
                piece = landed[v][table[v, n, slab]].astype(jnp.float32)
                red = red + transmit * piece[0]
                green = green + transmit * piece[1]
                blue = blue + transmit * piece[2]
                transmit = transmit * (1.0 - piece[3])
            return red, green, blue, transmit

        zero = jnp.zeros((strip, lanes), jnp.float32)
        red, green, blue, transmit = lax.fori_loop(
            0, slabs, at_position, (zero, zero, zero, zero + 1.0)
        )
        out_ref[v, 0, 0] = red
        out_ref[v, 1, 0] = green
        out_ref[v, 2, 0] = blue
        out_ref[v, 3, 0] = 1.0 - transmit

    @pl.loop(0, slabs - 1)
    def _(i):
        peer = peer_at(i)
        a_copy(peer, me).wait_send()
        b_copy(peer, me).wait_send()
        for v in range(views):
            y_copy(v, peer, me).wait_send()

    for v in range(views):
        for step in STEPS:
            if step == 0:
                continue

            @pl.when((col + step >= 0) & (col + step < columns))
            def _(v=v, step=step):
                c_copy(v, step).wait_send()


def on_device(density, albedo, targets, offsets, slab_order):
    depth_cells, rows, lanes = density.shape
    views = slab_order.shape[0]
    slabs = lax.axis_size("depth")
    columns = lax.axis_size("col")
    strip = rows // slabs
    terms = sum(len(shear_plan(shear, depth_cells)[1]) for shear in SHEARS)
    f32, bf16 = jnp.float32, jnp.bfloat16
    dma = pltpu.SemaphoreType.DMA
    return pl.pallas_call(
        functools.partial(kernel, (slabs, columns, depth_cells, rows, lanes)),
        out_shape=jax.ShapeDtypeStruct((views, 4, 1, strip, lanes), f32),
        in_specs=[
            pl.BlockSpec(memory_space=pl.ANY),
            pl.BlockSpec(memory_space=pl.ANY),
            pl.BlockSpec(memory_space=pltpu.SMEM),
            pl.BlockSpec(memory_space=pltpu.SMEM),
            pl.BlockSpec(memory_space=pltpu.SMEM),
        ],
        out_specs=pl.BlockSpec(memory_space=pltpu.VMEM),
        scratch_shapes=[
            pltpu.VMEM((depth_cells, rows, lanes), f32),
            pltpu.VMEM((3, depth_cells, rows, lanes), bf16),
            pltpu.VMEM((slabs, strip, lanes), f32),
            pltpu.VMEM((slabs, strip, lanes), f32),
            pltpu.VMEM((slabs, strip, lanes), f32),
            pltpu.VMEM((slabs, strip, lanes), f32),
            pltpu.VMEM((terms, 3, rows, lanes), f32),
            pltpu.VMEM((views, slabs, 4, strip, lanes), bf16),
            pltpu.VMEM((slabs, 4, strip, lanes), bf16),
            pltpu.VMEM((slabs, 4, strip, lanes), bf16),
            pltpu.VMEM((views, SLOTS, 4, strip, lanes), bf16),
            pltpu.VMEM((SLOTS + 1, 4, strip, lanes), bf16),
            pltpu.VMEM((SLOTS + 1, 4, strip, lanes), bf16),
            pltpu.SMEM((views, len(STEPS), slabs), jnp.int32),
            dma((2,)),
            dma((slabs,)),
            dma((slabs,)),
            dma((slabs,)),
            dma((slabs,)),
            dma((views, slabs)),
            dma((views, slabs)),
            dma((views, len(STEPS))),
            dma((views, len(STEPS))),
        ],
        compiler_params=pltpu.CompilerParams(collective_id=0, has_side_effects=True),
    )(density, albedo, targets, offsets.transpose(0, 2, 3, 1), slab_order)


def solution(mesh):
    in_specs = (
        P("depth", "row", "col"),
        P(None, "depth", "row", "col"),
        P(None, None, "row", None),
        P(None, None, "row", "col"),
        P(),
    )
    out_specs = P(None, None, "row", "depth", "col")
    return jax.shard_map(
        on_device, mesh=mesh, in_specs=in_specs, out_specs=out_specs, check_vma=False
    )
```

time: 89.8 us -> 37 us (0.41)
  the two profiles are of different devices: /device:TPU:196 before, /device:TPU:64 now
where the time goes in v1:
time: 37 us; the launch traced here: 36.7 us
  Pallas kernels  35.3 us (95%)
  local copies, waits for them, and re-layouts  1.47 us (4%)
    pallas_call x1, Pallas kernels, on_device(): pl.pallas_call(functools.partial(kernel, (slabs, columns, depth_cells, ro...  35.3 us
    unnamed x1, local copies, waits for them, and re-layouts  1.47 us

profile of v1, /device:TPU:64, one launch (start us, length us, event | category | flops | bytes accessed | tf_op | source)
XLA Modules:
  0.0 36.7 jit_solution(2842700904582967701)
XLA Ops:
  0.0 35.3 %shard_map.55 = f32[2,4,1,16,128]{4,3,2,1,0:T(8,128)} custom-call(f32[16,128,128]{2,1,0:T(8,128)} %density_hbm.1, bf16[3,16,128,128]{3,2,1,0:T(8,128)(2,1)} %albedo_hbm.1, s32[2,8,1,48]{3,2,1,0:T(1,128)} %targets.1, s32[2,1,1,8]{3,2,1,0:T(1,128)} %bitcast.3, s32[2,8]{1,0:T(2,128)} %slab_order.1), custom_call_target="tpu_custom_call" | custom-call | tf_op jit(solution)/shard_map/pallas_call | solution.py:360
  35.3 1.5 %copy.8 = f32[2,4,1,16,128]{4,3,2,1,0:T(8,128)} copy(f32[2,4,1,16,128]{4,3,2,1,0:T(8,128)} %shard_map.55) | data formatting | bytes 131072

commit v2 on v1

v2 whole, which is shorter than its diff:
```python
import functools
import math

import jax
import jax.numpy as jnp
from jax import lax
from jax.experimental import pallas as pl
from jax.experimental.pallas import tpu as pltpu
from jax.sharding import PartitionSpec as P

SHEARS = (0.3125, -0.4375)
BRIGHTNESS = 4.0
LOGICAL = pl.DeviceIdType.LOGICAL
MIDDLE = 0.29

STEPS = (-1, 0, 1, 2, 3, 4)
SLOT_COUNT = {-1: 2, 0: 4, 1: 4, 2: 4, 3: 4, 4: 2}
SLOT_BASE = {-1: 0, 0: 2, 1: 6, 2: 10, 3: 14, 4: 18}
SLOTS = 20
EMPTY = 20
EARLY = 4
UNROLL = 2


def shear_plan(shear, depth_cells):
    plan = []
    for z in range(depth_cells):
        whole = math.floor(shear * z)
        plan.append((whole, shear * z - whole))
    terms = sorted({k + e for k, f in plan for e in (0, 1) if e == 0 or f > 0})
    return plan, terms


def kernel(
    sizes,
    density_hbm,
    albedo_hbm,
    targets_hbm,
    offsets_hbm,
    order_hbm,
    out_ref,
    targets,
    offsets,
    slab_order,
    dens,
    alb,
    depth_strips,
    depth_seen,
    light_strips,
    light,
    partial,
    images,
    veils,
    strips_a,
    strips_b,
    veil_strips,
    outgoing,
    veil_outgoing,
    landed_a,
    landed_b,
    veil_landed,
    table,
    picks,
    density_sems,
    load_sems,
    a_send,
    a_recv,
    b_send,
    b_recv,
    o_send,
    o_recv,
    y_send,
    y_recv,
    c_send,
    c_recv,
):
    slabs, columns, depth_cells, rows, lanes = sizes
    views = len(SHEARS)
    strips, landed = (strips_a, strips_b), (landed_a, landed_b)
    strip = rows // slabs
    plans = [shear_plan(shear, depth_cells) for shear in SHEARS]
    firsts = [0, len(plans[0][1])]
    me = lax.axis_index("depth")
    col = lax.axis_index("col")
    layer = lax.axis_size("row") * columns
    here = me * layer + lax.axis_index("row") * columns + col

    def device(peer):
        return here + (peer - me) * layer


    barrier = pltpu.get_barrier_semaphore()
    for hop in range(1, slabs):
        pl.semaphore_signal(
            barrier,
            inc=1,
            device_id=device(lax.rem(me + hop, slabs)),
            device_id_type=LOGICAL,
        )
    for hop in (-4, -3, -2, -1, 1, 2, 3, 4):

        @pl.when((col + hop >= 0) & (col + hop < columns))
        def _(hop=hop):
            pl.semaphore_signal(barrier, inc=1, device_id=here + hop, device_id_type=LOGICAL)

    lane = lax.broadcasted_iota(jnp.int32, (strip, lanes), 1)

    def strip_rows(p):
        return pl.ds(pl.multiple_of(p * strip, strip), strip)

    def peer_at(i):
        half, sign = (i + 1) // 2, 1 - 2 * (i % 2)
        return lax.rem(me + slabs // 2 + sign * half, slabs)

    def density_load(i):
        at = strip_rows(peer_at(i))
        return pltpu.make_async_copy(density_hbm.at[:, at], dens.at[:, at], density_sems.at[i])

    @pl.loop(0, slabs)
    def _(i):
        density_load(i).start()

    load_small = [
        pltpu.make_async_copy(src, dst, load_sems.at[n])
        for n, (src, dst) in enumerate(
            ((offsets_hbm, offsets), (targets_hbm, targets), (order_hbm, slab_order))
        )
    ]
    for load in load_small:
        load.start()
    load_albedo = pltpu.make_async_copy(albedo_hbm, alb, load_sems.at[3])
    load_albedo.start()

    neighbours = jnp.minimum(col, 4) + jnp.minimum(columns - 1 - col, 4)
    pl.semaphore_wait(barrier, slabs - 1 + neighbours)

    def depth_copy(src, dst, send_sem, recv_sem, peer):
        return pltpu.make_async_remote_copy(
            src_ref=src,
            dst_ref=dst,
            send_sem=send_sem,
            recv_sem=recv_sem,
            device_id=device(peer),
            device_id_type=LOGICAL,
        )

    def all_peers(src, dst, send_sem, recv_sem):
        span = pl.ds(0, slabs - 1)
        return depth_copy(src.at[span], dst.at[span], send_sem, recv_sem, me)

    def a_copy(peer, source):
        return depth_copy(depth_strips.at[peer], depth_seen.at[source], a_send, a_recv, peer)

    def b_copy(peer, source):
        return depth_copy(light_strips.at[peer], light.at[source], b_send, b_recv, peer)

    def all_a():
        return all_peers(depth_strips, depth_seen, a_send, a_recv)

    def all_b():
        return all_peers(light_strips, light, b_send, b_recv)

    @pl.loop(0, slabs)
    def _(i):
        p = peer_at(i)
        density_load(i).wait()
        total = jnp.sum(dens[:, strip_rows(p), :], axis=0)
        depth_strips[p] = (total - MIDDLE).astype(jnp.bfloat16)

        @pl.when(i < slabs - 1)
        def _():
            a_copy(p, me).start()

    depth_seen[me] = depth_strips[me]
    for load in load_small:
        load.wait()
    load_albedo.wait()

    def lane_mask(shift, weight):
        inside = (lane >= shift) if shift >= 0 else (lane < lanes + shift)
        return jnp.where(inside, jnp.float32(weight), jnp.float32(0.0))

    def rolled(value, shift):
        return value if shift % lanes == 0 else pltpu.roll(value, shift % lanes, 1)

    def o_copy(peer, source):
        return depth_copy(veils.at[peer], veil_strips.at[source], o_send, o_recv, peer)

    def composite(i):
        p = peer_at(i)
        at = strip_rows(p)
        inside = jnp.ones((strip, lanes), jnp.float32)
        transmit = [jnp.ones((strip, lanes), jnp.float32) for _ in range(views)]
        sums = [{} for _ in range(views)]
        for z in range(depth_cells):
            through = jnp.exp(-dens[z, at, :])
            opacity = 1.0 - through
            lit = (BRIGHTNESS * inside) * opacity
            inside = inside * through
            colour = [alb[c, z, at, :].astype(jnp.float32) * lit for c in range(3)]
            for v in range(views):
                whole, fraction = plans[v][0][z]
                moved = None
                for k, weight in ((whole, 1.0 - fraction), (whole + 1, fraction)):
                    if weight == 0.0:
                        continue
                    part = lane_mask(k, weight) * rolled(opacity, k)
                    moved = part if moved is None else moved + part
                    seen = transmit[v] if z else None
                    seen = lane_mask(-k, weight) * (
                        rolled(seen, -k) if z else jnp.ones((strip, lanes), jnp.float32)
                    )
                    terms = [seen * colour[c] for c in range(3)]
                    if k in sums[v]:
                        terms = [old + new for old, new in zip(sums[v][k], terms)]
                    sums[v][k] = terms
                transmit[v] = transmit[v] * (1.0 - moved)
                later = {
                    k for w, f in plans[v][0][z + 1 :] for k in ((w, w + 1) if f else (w,))
                }
                for k in [k for k in sums[v] if k not in later]:
                    for c in range(3):
                        partial[firsts[v] + plans[v][1].index(k), c, at, :] = sums[v][k][c]
                    del sums[v][k]
        for v in range(views):
            image = pltpu.roll(1.0 - transmit[v], offsets[v, 0, 0, me], 1)
            veils[p, v] = image.astype(jnp.bfloat16)

        @pl.when(i < slabs - 1)
        def _():
            o_copy(p, me).start()

    pl.loop(0, EARLY)(composite)
    all_a().wait_recv()
    before = jnp.zeros((strip, lanes), jnp.float32)
    for d in range(slabs):
        light_strips[d] = jnp.exp(-before).astype(jnp.bfloat16)
        before = before + (depth_seen[d].astype(jnp.float32) + MIDDLE)

    @pl.loop(0, slabs - 1)
    def _(i):
        b_copy(peer_at(i), me).start()

    light[me] = light_strips[me]
    pl.loop(EARLY, slabs)(composite)
    veil_strips[me] = veils[me]

    for v in range(views):
        rel = [targets[v, d, 0, col] - col for d in range(slabs)]
        for n, step in enumerate(STEPS[:-1]):
            first = jnp.int32(slabs)
            second = jnp.int32(-1)
            for d in range(slabs):
                match = rel[d] == step
                first = jnp.where(match, jnp.minimum(first, d), first)
                second = jnp.where(match, d, second)
            valid = second >= 0
            for member, slab in ((0, first), (1, second)):
                slab = jnp.where(valid, slab, 0)
                start = offsets[v, 0, 0, slab]
                picks[v, n, member, 0] = slab
                picks[v, n, member, 1] = jnp.where(valid, start, lanes)
                picks[v, n, member, 2] = jnp.where(valid, start, 0)

    for v in range(views):
        for n, step in enumerate(STEPS):
            source = col - step
            present = (source >= 0) & (source < columns)
            source = jnp.clip(source, 0, columns - 1)
            rel = [targets[v, d, 0, source] - source for d in range(slabs)]
            for d in range(slabs):
                second = functools.reduce(
                    jnp.logical_or, [rel[e] == rel[d] for e in range(d)], False
                )
                member = jnp.where(second, 1, 0)
                slot = jnp.int32(EMPTY)
                if step < 4:
                    slot = jnp.where(rel[d] == step, SLOT_BASE[step] + member, slot)
                if step > -1:
                    after = SLOT_BASE[step] + (2 if step < 4 else 0)
                    slot = jnp.where(rel[d] == step - 1, after + member, slot)
                table[v, n, d] = jnp.where(present, slot, EMPTY)

    all_b().wait_recv()

    def y_copy(v, peer, source):
        return depth_copy(
            images.at[v, peer], strips[v].at[source], y_send.at[v], y_recv.at[v], peer
        )

    def all_o():
        return all_peers(veils, veil_strips, o_send, o_recv)

    def all_y(v):
        return all_peers(images.at[v], strips[v], y_send.at[v], y_recv.at[v])

    for v in range(views):

        @pl.loop(0, slabs, unroll=UNROLL)
        def _(i, v=v):
            p = peer_at(i)
            at = strip_rows(p)
            front_light = light[p].astype(jnp.float32)
            for c in range(3):
                total = None
                for n, k in enumerate(plans[v][1]):
                    part = rolled(front_light * partial[firsts[v] + n, c, at, :], k)
                    total = part if total is None else total + part
                total = pltpu.roll(total, offsets[v, 0, 0, me], 1)
                images[v, p, c] = total.astype(jnp.bfloat16)

            @pl.when(i < slabs - 1)
            def _():
                y_copy(v, p, me).start()

        strips[v][me] = images[v, me]

    def slot_copy(src, dst, send, recv, step):
        span = pl.ds(SLOT_BASE[step], SLOT_COUNT[step])
        n = STEPS.index(step)
        return pltpu.make_async_remote_copy(
            src_ref=src.at[span],
            dst_ref=dst.at[span],
            send_sem=send.at[n],
            recv_sem=recv.at[n],
            device_id=here + step,
            device_id_type=LOGICAL,
        )

    def c_copy(v, step):
        if v == views:
            src, dst = veil_outgoing, veil_landed
        else:
            src, dst = outgoing.at[v], landed[v]
        return slot_copy(src, dst, c_send.at[v], c_recv.at[v], step)

    def send_to(v, step):
        if step == 0:
            return

        @pl.when((col + step >= 0) & (col + step < columns))
        def _():
            c_copy(v, step).start()

    def await_from(v):
        for step in STEPS:
            if step == 0:
                continue

            @pl.when((col - step >= 0) & (col - step < columns))
            def _(step=step):
                c_copy(v, step).wait_recv()

    def place(v, n, put_left, put_right, read):
        step = STEPS[n]
        after = step + 1
        for member in (0, 1):
            piece = read(picks[v, n, member, 0])
            left = jnp.where(lane >= picks[v, n, member, 1], 1.0, 0.0).astype(jnp.bfloat16)
            right = jnp.where(lane < picks[v, n, member, 2], 1.0, 0.0).astype(jnp.bfloat16)
            put_left(step == 0, SLOT_BASE[step] + member, piece * left)
            put_right(
                after == 0, SLOT_BASE[after] + (2 if after < 4 else 0) + member, piece * right
            )

    ORDER = (4, 3, 2, 1, 0)

    all_o().wait_recv()

    for n in ORDER:
        for v in range(views):

            def put(own, slot, value, v=v):
                (veil_landed if own else veil_outgoing)[slot, v] = value

            place(v, n, put, put, lambda slab, v=v: veil_strips[slab, v])
        send_to(views, STEPS[n] + 1)
    send_to(views, -1)
    veil_landed[EMPTY] = jnp.zeros(veil_landed.shape[1:], jnp.bfloat16)

    for v in range(views):
        landed[v][EMPTY] = jnp.zeros(landed[v].shape[1:], jnp.bfloat16)

        all_y(v).wait_recv()

        for n in ORDER:

            def put(own, slot, value, v=v):
                if own:
                    landed[v][slot] = value
                else:
                    outgoing[v, slot] = value

            place(v, n, put, put, lambda slab, v=v: strips[v][slab])
            send_to(v, STEPS[n] + 1)
        send_to(v, -1)

    all_a().wait_send()
    all_b().wait_send()
    all_o().wait_send()
    for v in range(views):
        all_y(v).wait_send()

    await_from(views)
    for v in range(views):
        await_from(v)
        if v == views - 1:
            for w in range(views + 1):
                for step in STEPS:
                    if step == 0:
                        continue

                    @pl.when((col + step >= 0) & (col + step < columns))
                    def _(w=w, step=step):
                        c_copy(w, step).wait_send()

        def at_position(position, state, v=v):
            slab = slab_order[v, position]
            red, green, blue, transmit = state
            for n in reversed(range(len(STEPS))):
                slot = table[v, n, slab]
                piece = landed[v][slot].astype(jnp.float32)
                red = red + transmit * piece[0]
                green = green + transmit * piece[1]
                blue = blue + transmit * piece[2]
                veil = veil_landed[slot, v].astype(jnp.float32)
                transmit = transmit * (1.0 - veil)
            return red, green, blue, transmit

        zero = jnp.zeros((strip, lanes), jnp.float32)
        red, green, blue, transmit = lax.fori_loop(
            0, slabs, at_position, (zero, zero, zero, zero + 1.0), unroll=2
        )
        out_ref[v, 0, 0] = red
        out_ref[v, 1, 0] = green
        out_ref[v, 2, 0] = blue
        out_ref[v, 3, 0] = 1.0 - transmit


def on_device(density, albedo, targets, offsets, slab_order):
    depth_cells, rows, lanes = density.shape
    views = slab_order.shape[0]
    slabs = lax.axis_size("depth")
    columns = lax.axis_size("col")
    strip = rows // slabs
    terms = sum(len(shear_plan(shear, depth_cells)[1]) for shear in SHEARS)
    f32, bf16 = jnp.float32, jnp.bfloat16
    dma = pltpu.SemaphoreType.DMA
    return pl.pallas_call(
        functools.partial(kernel, (slabs, columns, depth_cells, rows, lanes)),
        out_shape=pltpu.VMEM((views, 4, 1, strip, lanes), f32),
        in_specs=[
            pl.BlockSpec(memory_space=pl.ANY),
            pl.BlockSpec(memory_space=pl.ANY),
            pl.BlockSpec(memory_space=pl.ANY),
            pl.BlockSpec(memory_space=pl.ANY),
            pl.BlockSpec(memory_space=pl.ANY),
        ],
        out_specs=pl.BlockSpec(memory_space=pltpu.VMEM),
        scratch_shapes=[
            pltpu.SMEM((views, slabs, 1, columns), jnp.int32),
            pltpu.SMEM((views, 1, 1, slabs), jnp.int32),
            pltpu.SMEM((views, slabs), jnp.int32),
            pltpu.VMEM((depth_cells, rows, lanes), f32),
            pltpu.VMEM((3, depth_cells, rows, lanes), bf16),
            pltpu.VMEM((slabs, strip, lanes), bf16),
            pltpu.VMEM((slabs, strip, lanes), bf16),
            pltpu.VMEM((slabs, strip, lanes), bf16),
            pltpu.VMEM((slabs, strip, lanes), bf16),
            pltpu.VMEM((terms, 3, rows, lanes), f32),
            pltpu.VMEM((views, slabs, 3, strip, lanes), bf16),
            pltpu.VMEM((slabs, views, strip, lanes), bf16),
            pltpu.VMEM((slabs, 3, strip, lanes), bf16),
            pltpu.VMEM((slabs, 3, strip, lanes), bf16),
            pltpu.VMEM((slabs, views, strip, lanes), bf16),
            pltpu.VMEM((views, SLOTS, 3, strip, lanes), bf16),
            pltpu.VMEM((SLOTS, views, strip, lanes), bf16),
            pltpu.VMEM((SLOTS + 1, 3, strip, lanes), bf16),
            pltpu.VMEM((SLOTS + 1, 3, strip, lanes), bf16),
            pltpu.VMEM((SLOTS + 1, views, strip, lanes), bf16),
            pltpu.SMEM((views, len(STEPS), slabs), jnp.int32),
            pltpu.SMEM((views, len(STEPS) - 1, 2, 3), jnp.int32),
            dma((slabs,)),
            dma((4,)),
            dma,
            dma,
            dma,
            dma,
            dma,
            dma,
            dma((views,)),
            dma((views,)),
            dma((views + 1, len(STEPS))),
            dma((views + 1, len(STEPS))),
        ],
        compiler_params=pltpu.CompilerParams(collective_id=0, has_side_effects=True),
    )(density, albedo, targets, offsets.transpose(0, 2, 3, 1), slab_order)


def solution(mesh):
    in_specs = (
        P("depth", "row", "col"),
        P(None, "depth", "row", "col"),
        P(None, None, "row", None),
        P(None, None, "row", "col"),
        P(),
    )
    out_specs = P(None, None, "row", "depth", "col")
    return jax.shard_map(
        on_device, mesh=mesh, in_specs=in_specs, out_specs=out_specs, check_vma=False
    )
```

time: 37 us -> 32.8 us (0.89)
  the two profiles are of different devices: /device:TPU:64 before, /device:TPU:2 now
where the time goes in v2:
time: 32.8 us; the launch traced here: 32.7 us
  Pallas kernels  32 us (98%)
  local copies, waits for them, and re-layouts  0.63 us (2%)
    pallas_call x1, Pallas kernels, on_device(): pl.pallas_call(functools.partial(kernel, (slabs, columns, depth_cells, ro...  32 us

profile of v2, /device:TPU:2, one launch (start us, length us, event | category | flops | bytes accessed | tf_op | source)
XLA Modules:
  0.0 32.7 jit_solution(11884017633816434347)
XLA Ops:
  0.0 32.0 %shard_map.55 = f32[2,4,1,16,128]{4,3,2,1,0:T(8,128)S(1)} custom-call(f32[16,128,128]{2,1,0:T(8,128)} %density_hbm.1, bf16[3,16,128,128]{3,2,1,0:T(8,128)(2,1)} %albedo_hbm.1, s32[2,8,1,48]{3,2,1,0:T(1,128)} %targets_hbm.1, s32[2,1,1,8]{3,2,1,0:T(1,128)} %bitcast.3, s32[2,8]{1,0:T(2,128)} %order_hbm.1), custom_call_target="tpu_custom_call" | custom-call | tf_op jit(solution)/shard_map/pallas_call | solution.py:449
  32.0 0.6 %copy.8 = f32[2,4,1,16,128]{4,3,2,1,0:T(8,128)} copy(f32[2,4,1,16,128]{4,3,2,1,0:T(8,128)S(1)} %shard_map.55) | data formatting | bytes 131072

commit v3 on v2

--- a/solution.py
+++ b/solution.py
@@ -11,15 +11,15 @@
 SHEARS = (0.3125, -0.4375)
 BRIGHTNESS = 4.0
 LOGICAL = pl.DeviceIdType.LOGICAL
-MIDDLE = 0.29
+FAR_FIRST = (4, 3, 5, 2, 6, 1, 7)
 
 STEPS = (-1, 0, 1, 2, 3, 4)
 SLOT_COUNT = {-1: 2, 0: 4, 1: 4, 2: 4, 3: 4, 4: 2}
 SLOT_BASE = {-1: 0, 0: 2, 1: 6, 2: 10, 3: 14, 4: 18}
 SLOTS = 20
-EMPTY = 20
-EARLY = 4
-UNROLL = 2
+LAND_BASE = {-1: 0, 0: 3, 1: 8, 2: 13, 3: 18, 4: 23}
+LAND_SLOTS = 26
+EARLY = 3
 
 
 def shear_plan(shear, depth_cells):
@@ -59,6 +59,7 @@
     landed_a,
     landed_b,
     veil_landed,
+    weights,
     table,
     picks,
     density_sems,
@@ -90,7 +91,7 @@
 
 
     barrier = pltpu.get_barrier_semaphore()
-    for hop in range(1, slabs):
+    for hop in FAR_FIRST:
         pl.semaphore_signal(
             barrier,
             inc=1,
@@ -131,6 +132,12 @@
     load_albedo = pltpu.make_async_copy(albedo_hbm, alb, load_sems.at[3])
     load_albedo.start()
 
+    for n, step in enumerate(STEPS):
+        count = SLOT_COUNT[step]
+        for v in range(views):
+            landed[v][n][count] = jnp.zeros(landed[v][n].shape[1:], jnp.bfloat16)
+        veil_landed[LAND_BASE[step] + count] = jnp.zeros(veil_landed.shape[1:], jnp.bfloat16)
+
     neighbours = jnp.minimum(col, 4) + jnp.minimum(columns - 1 - col, 4)
     pl.semaphore_wait(barrier, slabs - 1 + neighbours)
 
@@ -152,20 +159,22 @@
         return depth_copy(depth_strips.at[peer], depth_seen.at[source], a_send, a_recv, peer)
 
     def b_copy(peer, source):
-        return depth_copy(light_strips.at[peer], light.at[source], b_send, b_recv, peer)
+        return depth_copy(
+            light_strips.at[peer], light.at[source], b_send, b_recv.at[source], peer
+        )
 
     def all_a():
         return all_peers(depth_strips, depth_seen, a_send, a_recv)
 
     def all_b():
-        return all_peers(light_strips, light, b_send, b_recv)
+        return all_peers(light_strips, light, b_send, b_recv.at[0])
 
     @pl.loop(0, slabs)
     def _(i):
         p = peer_at(i)
         density_load(i).wait()
         total = jnp.sum(dens[:, strip_rows(p), :], axis=0)
-        depth_strips[p] = (total - MIDDLE).astype(jnp.bfloat16)
+        depth_strips[p] = total
 
         @pl.when(i < slabs - 1)
         def _():
@@ -234,8 +243,8 @@
     all_a().wait_recv()
     before = jnp.zeros((strip, lanes), jnp.float32)
     for d in range(slabs):
-        light_strips[d] = jnp.exp(-before).astype(jnp.bfloat16)
-        before = before + (depth_seen[d].astype(jnp.float32) + MIDDLE)
+        light_strips[d] = jnp.exp(-before)
+        before = before + depth_seen[d]
 
     @pl.loop(0, slabs - 1)
     def _(i):
@@ -268,20 +277,18 @@
             present = (source >= 0) & (source < columns)
             source = jnp.clip(source, 0, columns - 1)
             rel = [targets[v, d, 0, source] - source for d in range(slabs)]
+            empty = SLOT_COUNT[step]
             for d in range(slabs):
                 second = functools.reduce(
                     jnp.logical_or, [rel[e] == rel[d] for e in range(d)], False
                 )
                 member = jnp.where(second, 1, 0)
-                slot = jnp.int32(EMPTY)
+                slot = jnp.int32(empty)
                 if step < 4:
-                    slot = jnp.where(rel[d] == step, SLOT_BASE[step] + member, slot)
+                    slot = jnp.where(rel[d] == step, member, slot)
                 if step > -1:
-                    after = SLOT_BASE[step] + (2 if step < 4 else 0)
-                    slot = jnp.where(rel[d] == step - 1, after + member, slot)
-                table[v, n, d] = jnp.where(present, slot, EMPTY)
-
-    all_b().wait_recv()
+                    slot = jnp.where(rel[d] == step - 1, member + (2 if step < 4 else 0), slot)
+                table[v, n, d] = jnp.where(present, slot, empty)
 
     def y_copy(v, peer, source):
         return depth_copy(
@@ -294,20 +301,27 @@
     def all_y(v):
         return all_peers(images.at[v], strips[v], y_send.at[v], y_recv.at[v])
 
-    for v in range(views):
-
-        @pl.loop(0, slabs, unroll=UNROLL)
+    def colours(v, p):
+        at = strip_rows(p)
+        front_light = light[p]
+        for c in range(3):
+            total = None
+            for n, k in enumerate(plans[v][1]):
+                part = rolled(front_light * partial[firsts[v] + n, c, at, :], k)
+                total = part if total is None else total + part
+            total = pltpu.roll(total, offsets[v, 0, 0, me], 1)
+            images[v, p, c] = total.astype(jnp.bfloat16)
+
+    @pl.loop(0, slabs - 1)
+    def _(i):
+        b_copy(me, peer_at(i)).wait_recv()
+
+    for v in range(views):
+
+        @pl.loop(0, slabs, unroll=2)
         def _(i, v=v):
             p = peer_at(i)
-            at = strip_rows(p)
-            front_light = light[p].astype(jnp.float32)
-            for c in range(3):
-                total = None
-                for n, k in enumerate(plans[v][1]):
-                    part = rolled(front_light * partial[firsts[v] + n, c, at, :], k)
-                    total = part if total is None else total + part
-                total = pltpu.roll(total, offsets[v, 0, 0, me], 1)
-                images[v, p, c] = total.astype(jnp.bfloat16)
+            colours(v, p)
 
             @pl.when(i < slabs - 1)
             def _():
@@ -315,25 +329,22 @@
 
         strips[v][me] = images[v, me]
 
-    def slot_copy(src, dst, send, recv, step):
-        span = pl.ds(SLOT_BASE[step], SLOT_COUNT[step])
-        n = STEPS.index(step)
+    def c_copy(v, step):
+        n, count = STEPS.index(step), SLOT_COUNT[step]
+        span = pl.ds(SLOT_BASE[step], count)
+        if v == views:
+            src, dst = veil_outgoing.at[span], veil_landed.at[pl.ds(LAND_BASE[step], count)]
+        else:
+            src, dst = outgoing.at[v, span], landed[v][n].at[pl.ds(0, count)]
         return pltpu.make_async_remote_copy(
-            src_ref=src.at[span],
-            dst_ref=dst.at[span],
-            send_sem=send.at[n],
-            recv_sem=recv.at[n],
+            src_ref=src,
+            dst_ref=dst,
+            send_sem=c_send.at[v, n],
+            recv_sem=c_recv.at[v, n],
             device_id=here + step,
             device_id_type=LOGICAL,
         )
 
-    def c_copy(v, step):
-        if v == views:
-            src, dst = veil_outgoing, veil_landed
-        else:
-            src, dst = outgoing.at[v], landed[v]
-        return slot_copy(src, dst, c_send.at[v], c_recv.at[v], step)
-
     def send_to(v, step):
         if step == 0:
             return
@@ -342,14 +353,13 @@
         def _():
             c_copy(v, step).start()
 
-    def await_from(v):
-        for step in STEPS:
-            if step == 0:
-                continue
-
-            @pl.when((col - step >= 0) & (col - step < columns))
-            def _(step=step):
-                c_copy(v, step).wait_recv()
+    def await_from(v, step):
+        if step == 0:
+            return
+
+        @pl.when((col - step >= 0) & (col - step < columns))
+        def _():
+            c_copy(v, step).wait_recv()
 
     def place(v, n, put_left, put_right, read):
         step = STEPS[n]
@@ -358,42 +368,39 @@
             piece = read(picks[v, n, member, 0])
             left = jnp.where(lane >= picks[v, n, member, 1], 1.0, 0.0).astype(jnp.bfloat16)
             right = jnp.where(lane < picks[v, n, member, 2], 1.0, 0.0).astype(jnp.bfloat16)
-            put_left(step == 0, SLOT_BASE[step] + member, piece * left)
-            put_right(
-                after == 0, SLOT_BASE[after] + (2 if after < 4 else 0) + member, piece * right
-            )
-
-    ORDER = (4, 3, 2, 1, 0)
+            put_left(step, member, piece * left)
+            put_right(after, member + (2 if after < 4 else 0), piece * right)
+
+    ORDER = ((3, ()), (2, (2,)), (4, (3, 4)), (1, (1,)), (0, (-1,)))
 
     all_o().wait_recv()
 
-    for n in ORDER:
+    for n, ready in ORDER:
         for v in range(views):
 
-            def put(own, slot, value, v=v):
-                (veil_landed if own else veil_outgoing)[slot, v] = value
+            def put(step, slot, value, v=v):
+                if step == 0:
+                    veil_landed[LAND_BASE[step] + slot, v] = value
+                else:
+                    veil_outgoing[SLOT_BASE[step] + slot, v] = value
 
             place(v, n, put, put, lambda slab, v=v: veil_strips[slab, v])
-        send_to(views, STEPS[n] + 1)
-    send_to(views, -1)
-    veil_landed[EMPTY] = jnp.zeros(veil_landed.shape[1:], jnp.bfloat16)
-
-    for v in range(views):
-        landed[v][EMPTY] = jnp.zeros(landed[v].shape[1:], jnp.bfloat16)
-
+        for step in ready:
+            send_to(views, step)
+    for v in range(views):
         all_y(v).wait_recv()
 
-        for n in ORDER:
-
-            def put(own, slot, value, v=v):
-                if own:
-                    landed[v][slot] = value
+        for n, ready in ORDER:
+
+            def put(step, slot, value, v=v):
+                if step == 0:
+                    landed[v][STEPS.index(step)][slot] = value
                 else:
-                    outgoing[v, slot] = value
+                    outgoing[v, SLOT_BASE[step] + slot] = value
 
             place(v, n, put, put, lambda slab, v=v: strips[v][slab])
-            send_to(v, STEPS[n] + 1)
-        send_to(v, -1)
+            for step in ready:
+                send_to(v, step)
 
     all_a().wait_send()
     all_b().wait_send()
@@ -401,40 +408,45 @@
     for v in range(views):
         all_y(v).wait_send()
 
-    await_from(views)
-    for v in range(views):
-        await_from(v)
-        if v == views - 1:
-            for w in range(views + 1):
-                for step in STEPS:
-                    if step == 0:
-                        continue
-
-                    @pl.when((col + step >= 0) & (col + step < columns))
-                    def _(w=w, step=step):
-                        c_copy(w, step).wait_send()
-
-        def at_position(position, state, v=v):
+    for step in STEPS:
+        await_from(views, step)
+    for v in range(views):
+
+        def at_position(position, transmit, v=v):
             slab = slab_order[v, position]
-            red, green, blue, transmit = state
-            for n in reversed(range(len(STEPS))):
-                slot = table[v, n, slab]
-                piece = landed[v][slot].astype(jnp.float32)
-                red = red + transmit * piece[0]
-                green = green + transmit * piece[1]
-                blue = blue + transmit * piece[2]
-                veil = veil_landed[slot, v].astype(jnp.float32)
-                transmit = transmit * (1.0 - veil)
-            return red, green, blue, transmit
-
+            for n, step in reversed(list(enumerate(STEPS))):
+                weights[v, n, position] = transmit
+                veil = veil_landed[LAND_BASE[step] + table[v, n, slab], v]
+                transmit = transmit * (1.0 - veil.astype(jnp.float32))
+            return transmit
+
+        one = jnp.ones((strip, lanes), jnp.float32)
+        out_ref[v, 3, 0] = 1.0 - lax.fori_loop(0, slabs, at_position, one, unroll=2)
+
+    for w in range(views + 1):
+        for step in STEPS:
+            if step == 0:
+                continue
+
+            @pl.when((col + step >= 0) & (col + step < columns))
+            def _(w=w, step=step):
+                c_copy(w, step).wait_send()
+
+    for v in range(views):
         zero = jnp.zeros((strip, lanes), jnp.float32)
-        red, green, blue, transmit = lax.fori_loop(
-            0, slabs, at_position, (zero, zero, zero, zero + 1.0), unroll=2
-        )
-        out_ref[v, 0, 0] = red
-        out_ref[v, 1, 0] = green
-        out_ref[v, 2, 0] = blue
-        out_ref[v, 3, 0] = 1.0 - transmit
+        sums = (zero, zero, zero)
+        for step in (0, -1, 1, 4, 3, 2):
+            n = STEPS.index(step)
+            await_from(v, step)
+
+            def add_piece(position, sums, v=v, n=n):
+                piece = landed[v][n][table[v, n, slab_order[v, position]]].astype(jnp.float32)
+                weight = weights[v, n, position]
+                return tuple(total + weight * piece[c] for c, total in enumerate(sums))
+
+            sums = lax.fori_loop(0, slabs, add_piece, sums, unroll=8)
+        for c in range(3):
+            out_ref[v, c, 0] = sums[c]
 
 
 def on_device(density, albedo, targets, offsets, slab_order):
@@ -463,10 +475,10 @@
             pltpu.SMEM((views, slabs), jnp.int32),
             pltpu.VMEM((depth_cells, rows, lanes), f32),
             pltpu.VMEM((3, depth_cells, rows, lanes), bf16),
-            pltpu.VMEM((slabs, strip, lanes), bf16),
-            pltpu.VMEM((slabs, strip, lanes), bf16),
-            pltpu.VMEM((slabs, strip, lanes), bf16),
-            pltpu.VMEM((slabs, strip, lanes), bf16),
+            pltpu.VMEM((slabs, strip, lanes), f32),
+            pltpu.VMEM((slabs, strip, lanes), f32),
+            pltpu.VMEM((slabs, strip, lanes), f32),
+            pltpu.VMEM((slabs, strip, lanes), f32),
             pltpu.VMEM((terms, 3, rows, lanes), f32),
             pltpu.VMEM((views, slabs, 3, strip, lanes), bf16),
             pltpu.VMEM((slabs, views, strip, lanes), bf16),
@@ -475,9 +487,10 @@
             pltpu.VMEM((slabs, views, strip, lanes), bf16),
             pltpu.VMEM((views, SLOTS, 3, strip, lanes), bf16),
             pltpu.VMEM((SLOTS, views, strip, lanes), bf16),
-            pltpu.VMEM((SLOTS + 1, 3, strip, lanes), bf16),
-            pltpu.VMEM((SLOTS + 1, 3, strip, lanes), bf16),
-            pltpu.VMEM((SLOTS + 1, views, strip, lanes), bf16),
+            [pltpu.VMEM((SLOT_COUNT[step] + 1, 3, strip, lanes), bf16) for step in STEPS],
+            [pltpu.VMEM((SLOT_COUNT[step] + 1, 3, strip, lanes), bf16) for step in STEPS],
+            pltpu.VMEM((LAND_SLOTS, views, strip, lanes), bf16),
+            pltpu.VMEM((views, len(STEPS), slabs, strip, lanes), f32),
             pltpu.SMEM((views, len(STEPS), slabs), jnp.int32),
             pltpu.SMEM((views, len(STEPS) - 1, 2, 3), jnp.int32),
             dma((slabs,)),
@@ -485,7 +498,7 @@
             dma,
             dma,
             dma,
-            dma,
+            dma((slabs,)),
             dma,
             dma,
             dma((views,)),

time: 32.8 us -> 32.8 us (level)
  no operation moved by 1% of the time
where the time goes in v3:
time: 32.8 us; the launch traced here: 32.7 us
  Pallas kernels  32 us (98%)
  local copies, waits for them, and re-layouts  0.63 us (2%)
    pallas_call x1, Pallas kernels, on_device(): pl.pallas_call(functools.partial(kernel, (slabs, columns, depth_cells, ro...  32 us

profile of v3, /device:TPU:2, one launch (start us, length us, event | category | flops | bytes accessed | tf_op | source)
XLA Modules:
  0.0 32.7 jit_solution(14976282043514492181)
XLA Ops:
  0.0 32.0 %shard_map.55 = f32[2,4,1,16,128]{4,3,2,1,0:T(8,128)S(1)} custom-call(f32[16,128,128]{2,1,0:T(8,128)} %density_hbm.1, bf16[3,16,128,128]{3,2,1,0:T(8,128)(2,1)} %albedo_hbm.1, s32[2,8,1,48]{3,2,1,0:T(1,128)} %targets_hbm.1, s32[2,1,1,8]{3,2,1,0:T(1,128)} %bitcast.3, s32[2,8]{1,0:T(2,128)} %order_hbm.1), custom_call_target="tpu_custom_call" | custom-call | tf_op jit(solution)/shard_map/pallas_call | solution.py:461
  32.0 0.6 %copy.8 = f32[2,4,1,16,128]{4,3,2,1,0:T(8,128)} copy(f32[2,4,1,16,128]{4,3,2,1,0:T(8,128)S(1)} %shard_map.55) | data formatting | bytes 131072

commit v4 on v3

--- a/solution.py
+++ b/solution.py
@@ -246,8 +246,7 @@
         light_strips[d] = jnp.exp(-before)
         before = before + depth_seen[d]
 
-    @pl.loop(0, slabs - 1)
-    def _(i):
+    for i in range(slabs - 1):
         b_copy(peer_at(i), me).start()
 
     light[me] = light_strips[me]
@@ -312,8 +311,7 @@
             total = pltpu.roll(total, offsets[v, 0, 0, me], 1)
             images[v, p, c] = total.astype(jnp.bfloat16)
 
-    @pl.loop(0, slabs - 1)
-    def _(i):
+    for i in range(slabs - 1):
         b_copy(me, peer_at(i)).wait_recv()
 
     for v in range(views):

time: 32.8 us -> 32.8 us (level)
  no operation moved by 1% of the time
where the time goes in v4:
time: 32.8 us; the launch traced here: 32.6 us
  Pallas kernels  32 us (98%)
  local copies, waits for them, and re-layouts  0.63 us (2%)
    pallas_call x1, Pallas kernels, on_device(): pl.pallas_call(functools.partial(kernel, (slabs, columns, depth_cells, ro...  32 us

profile of v4, /device:TPU:2, one launch (start us, length us, event | category | flops | bytes accessed | tf_op | source)
XLA Modules:
  0.0 32.6 jit_solution(16632818128400513144)
XLA Ops:
  0.0 32.0 %shard_map.55 = f32[2,4,1,16,128]{4,3,2,1,0:T(8,128)S(1)} custom-call(f32[16,128,128]{2,1,0:T(8,128)} %density_hbm.1, bf16[3,16,128,128]{3,2,1,0:T(8,128)(2,1)} %albedo_hbm.1, s32[2,8,1,48]{3,2,1,0:T(1,128)} %targets_hbm.1, s32[2,1,1,8]{3,2,1,0:T(1,128)} %bitcast.3, s32[2,8]{1,0:T(2,128)} %order_hbm.1), custom_call_target="tpu_custom_call" | custom-call | tf_op jit(solution)/shard_map/pallas_call | solution.py:459
  32.0 0.6 %copy.8 = f32[2,4,1,16,128]{4,3,2,1,0:T(8,128)} copy(f32[2,4,1,16,128]{4,3,2,1,0:T(8,128)S(1)} %shard_map.55) | data formatting | bytes 131072
